TPU v7x, 32 devices: a whole 2x2x4 slice. The times are simulated.
32 devices in a mesh: grp: 4 (over x, core), env: 8 (over z, y).
Axes of the slice: x: 2, y: 2, z: 4, core: 2. Of those that a mesh axis runs over, the one named last changes fastest.
Arguments:
- wavefunction: bfloat16 [8192, 1024], P('grp', 'env'), may hold values from -6 to 6
- left_tiles: bfloat16 [512, 128, 128], P(('grp', 'env')), may hold values from -0.5 to 0.5
- right_tiles: bfloat16 [26, 1024, 128], P(None, 'env'), may hold values from -0.5 to 0.5
- term_source: int32 [512], P('grp'), may hold values from 0 to 63
- term_target: int32 [512], P('grp'), may hold values from 0 to 63
- right_index: int32 [512], P('grp'), may hold values from 0 to 25
- term_sector: int32 [512, 1], P('grp'), may hold values from 0 to 31; in each aligned block of 16 rows (0 to 15, 16 to 31, ...) at most 4 rows name the same one
- column_sector: int32 [8], replicated, may hold values from 0 to 31
Outputs:
- applied: bfloat16 [8192, 1024], P('grp', 'env')
Inputs may be any that keep to these rules, and one draw needn't show every extreme that they name: `term_sector`: within each aligned block of 16 terms (the terms of one device) no sector appears more than 4 times, and every sector appears somewhere.
All inputs are finite; a program needn't handle non-finite values.
Results may differ from a plain program's by a relative error of at most 0.009.
Values may be sent and summed in bfloat16 or wider, within the bound.
A program may use at most 64 MiB of HBM per device.

v0:
```python
import jax
import jax.numpy as jnp
from jax import lax
from jax.sharding import PartitionSpec as P

MAXS = 4


def contribute(
    running, left_pick, source_rows, target_rows, right_rows, kept_mask, blocks, right_tiles
):
    source_blocks = blocks[source_rows]
    block_product = jnp.einsum(
        "kab,kbc->kac", left_pick, source_blocks, preferred_element_type=jnp.float32
    ).astype(jnp.bfloat16)
    term_image = jnp.einsum(
        "kac,kcd->kad", block_product, right_tiles[right_rows], preferred_element_type=jnp.float32
    )
    term_image = term_image * kept_mask[:, None, None]
    return running.at[target_rows].add(term_image)


def shards(
    wavefunction,
    left_tiles,
    right_tiles,
    term_source,
    term_target,
    right_index,
    term_sector,
    column_sector,
):
    tile_size = left_tiles.shape[1]
    env_count = lax.axis_size("env")
    env_place = lax.axis_index("env")
    sectors = term_sector[:, 0]
    my_sector = column_sector[env_place]
    gathered = lax.all_gather(wavefunction, "grp", axis=0, tiled=True)
    block_count = gathered.shape[0] // tile_size
    blocks = gathered.reshape(block_count, tile_size, tile_size)
    running = jnp.zeros((block_count, tile_size, tile_size), jnp.float32)
    tiles_dev = left_tiles.shape[0]
    sector_grid = sectors.reshape(env_count, tiles_dev)
    own_sectors = sector_grid[env_place]
    outgoing_miss = (own_sectors[None, :] != column_sector[:, None]).astype(jnp.int32)
    outgoing_pick = jnp.argsort(outgoing_miss, axis=1, stable=True)[:, :MAXS]
    outgoing = left_tiles[outgoing_pick]
    incoming = lax.all_to_all(outgoing, "env", split_axis=0, concat_axis=0, tiled=True)
    incoming_miss = (sector_grid != my_sector).astype(jnp.int32)
    incoming_pick = jnp.argsort(incoming_miss, axis=1, stable=True)[:, :MAXS]
    chosen = (jnp.arange(env_count, dtype=jnp.int32)[:, None] * tiles_dev + incoming_pick).reshape(
        -1
    )
    kept_mask = (
        (1 - jnp.take_along_axis(incoming_miss, incoming_pick, axis=1))
        .reshape(-1)
        .astype(jnp.float32)
    )
    running = contribute(
        running,
        incoming.reshape(-1, tile_size, tile_size),
        term_source[chosen],
        term_target[chosen],
        right_index[chosen],
        kept_mask,
        blocks,
        right_tiles,
    )
    summed = lax.psum_scatter(
        running.reshape(block_count * tile_size, tile_size).astype(jnp.bfloat16),
        "grp",
        scatter_dimension=0,
        tiled=True,
    )
    return summed


def solution(mesh):
    placed = (
        P("grp", "env"),
        P(("grp", "env"), None, None),
        P(None, "env", None),
        P("grp"),
        P("grp"),
        P("grp"),
        P("grp", None),
        P(),
    )
    return jax.shard_map(
        shards, mesh=mesh, in_specs=placed, out_specs=P("grp", "env"), check_vma=False
    )
```

profile of v0, /device:TPU:0, one launch (start us, length us, event | category | flops | bytes accessed | tf_op | source)
XLA Modules:
  0.0 99.8 jit_solution(12645802424836200396)
XLA Ops:
  6.5 0.7 all-gather.2.cloned.1.call-update
  7.3 0.5 broadcast.147
  7.8 1.3 %reduce.3 = s32[128]{0:T(128)S(1)} reduce(s32[128,1]{0,1:T(1,128)} %param.14, s32[]{:T(128)} %broadcast.147), dimensions={1}, to_apply=%param.14.reduce_sub_computation.3 | reduce | bytes 1028 | tf_op args[6]
  9.2 0.7 compare_convert_fusion
  9.9 0.7 sort.32
  10.6 0.1 copy.13
  10.7 0.1 reshape.126
  10.8 2.7 %gather_fusion.1 = bf16[32,128,128]{2,1,0:T(8,128)(2,1)} fusion(bf16[16,128,128]{2,1,0:T(8,128)(2,1)} %param.9, s32[1024]{0:T(1024)S(1)} %pad_clamp_fusion.2), kind=kCustom, calls=%fused_computation.1 | custom fusion | bytes 2097280 | tf_op jit(solution)/shard_map/gather | solution.py:47
  13.5 7.3 %all-to-all-start = ((bf16[8,4,128,128]{3,2,1,0:T(8,128)(2,1)}), bf16[8,4,128,128]{3,2,1,0:T(8,128)(2,1)S(1)}, u32[]{:S(2)}, u32[]{:S(2)}) async-start(bf16[8,4,128,128]{3,2,1,0:T(8,128)(2,1)} %bitcast.5), calls=%async_computation | async-start | bytes 2097152 | tf_op jit(solution)/shard_map/all_to_all | solution.py:48
  20.9 0.6 dynamic_slice.6
  21.5 0.6 compare_convert_fusion.1
  22.2 0.7 sort.31
  22.9 0.1 copy.14
  23.0 0.1 reshape.164
  23.1 0.7 gather_fusion.6
  23.9 0.1 copy.15
  24.0 0.1 copy.16
  24.0 0.1 convert_element_type.29
  24.2 0.1 reshape.112
  24.3 0.7 gather_fusion.4
  25.0 0.7 gather_fusion.2
  25.7 0.7 gather_fusion
  26.5 1.7 %gather_fusion.5 = bf16[32,128,128]{2,1,0:T(8,128)(2,1)} fusion(bf16[26,128,128]{2,1,0:T(8,128)(2,1)S(1)} %copy-done, s32[1024]{0:T(1024)S(1)} %pad_clamp_fusion), kind=kCustom, calls=%fused_computation.5 | custom fusion | bytes 2097280 | tf_op jit(solution)/shard_map/gather | solution.py:17
  28.2 6.1 %all-gather.2.cloned.1.call-done = bf16[8192,128]{1,0:T(8,128)(2,1)} async-done(((bf16[2048,128]{1,0:T(8,128)(2,1)}), bf16[8192,128]{1,0:T(8,128)(2,1)}) %all-gather.2.cloned.1.call-update) | async-done | bytes 2097168 | tf_op jit(solution)/shard_map/all_gather | solution.py:38
  34.2 3.3 %gather_fusion.3 = bf16[32,128,128]{2,1,0:T(8,128)(2,1)} fusion(bf16[64,128,128]{2,1,0:T(8,128)(2,1)} %bitcast.31, s32[1024]{0:T(1024)S(1)} %pad_clamp_fusion.1), kind=kCustom, calls=%fused_computation.3 | custom fusion | bytes 2097280 | tf_op jit(solution)/shard_map/gather | solution.py:12
  37.5 9.1 %all-to-all-done = bf16[8,4,128,128]{3,2,1,0:T(8,128)(2,1)S(1)} async-done(((bf16[8,4,128,128]{3,2,1,0:T(8,128)(2,1)}), bf16[8,4,128,128]{3,2,1,0:T(8,128)(2,1)S(1)}, u32[]{:S(2)}, u32[]{:S(2)}) %all-to-all-start) | async-done | bytes 1048608 | tf_op jit(solution)/shard_map/all_to_all | solution.py:48
  46.6 1.0 copy-done.4
  47.6 2.6 %convolution_multiply_fusion = f32[32,128,128]{2,1,0:T(8,128)S(1)} fusion(bf16[32,128,128]{2,1,0:T(8,128)(2,1)} %gather_fusion.5, bf16[32,128,128]{2,1,0:T(8,128)(2,1)} %bitcast.30, bf16[32,128,128]{2,1,0:T(8,128)(2,1)} %gather_fusion.3, f32[32]{0:T(128)S(1)} %convert_element_type.29), kind=kOutput, calls=%fused_computation.8 | convolution fusion | flops 269484032 | bytes 5243008 | tf_op jit(solution)/shard_map/kac,kcd->kad/dot_general | solution.py:16
  50.2 2.4 %broadcast_in_dim.8 = f32[64,128,128]{2,1,0:T(8,128)} broadcast(f32[]{:T(128)} %constant.11.clone.1), dimensions={} | broadcast | bytes 4194308 | tf_op jit(solution)/shard_map/broadcast_in_dim | solution.py:41
  52.6 6.2 %scatter_fusion = f32[64,128,128]{2,1,0:T(8,128)} fusion(f32[64,128,128]{2,1,0:T(8,128)} %broadcast_in_dim.8, s32[32]{0:T(128)S(1)} %fusion.1, f32[32,128,128]{2,1,0:T(8,128)S(1)} %convolution_multiply_fusion), kind=kCustom, calls=%fused_computation.7 | custom fusion | flops 524288 | bytes 6291584 | tf_op jit(solution)/shard_map/scatter-add | solution.py:20
  58.8 3.9 %convert_element_type.30 = bf16[64,128,128]{2,1,0:T(8,128)(2,1)} convert(f32[64,128,128]{2,1,0:T(8,128)} %scatter_fusion) | non-fusion elementwise | flops 1048576 | bytes 6291456 | tf_op jit(solution)/shard_map/convert_element_type | solution.py:70
  62.7 30.2 %reduce-scatter.2.cloned.1.call-done = bf16[2048,128]{1,0:T(8,128)(2,1)} async-done(((bf16[8192,128]{1,0:T(8,128)(2,1)}), bf16[2048,128]{1,0:T(8,128)(2,1)}) %reduce-scatter.2.cloned.1.call-update) | async-done | bytes 524304 | tf_op jit(solution)/shard_map/reduce_scatter | solution.py:69
  (33 shorter events, 0.5 us)
Async XLA Ops:
  6.5 19.9 %copy-start = (bf16[26,128,128]{2,1,0:T(8,128)(2,1)S(1)}, bf16[26,128,128]{2,1,0:T(8,128)(2,1)}, u32[]{:S(2)}) copy-start(bf16[26,128,128]{2,1,0:T(8,128)(2,1)} %param.10) | copy-start | bytes 2555908
  6.5 27.7 %all-gather.2.cloned.1.call-start = ((), (), s32[]{:S(2)}) async-start(), calls=%async_computation.2 | async-start | bytes 2621440 | tf_op jit(solution)/shard_map/all_gather | solution.py:38
  10.8 10.1 %copy-start.5 = (s32[8]{0:T(128)S(1)}, s32[8]{0:T(128)}, u32[]{:S(2)}) copy-start(s32[8]{0:T(128)} %param.15) | copy-start | bytes 100
  13.5 33.1 %all-to-all-start = ((bf16[8,4,128,128]{3,2,1,0:T(8,128)(2,1)}), bf16[8,4,128,128]{3,2,1,0:T(8,128)(2,1)S(1)}, u32[]{:S(2)}, u32[]{:S(2)}) async-start(bf16[8,4,128,128]{3,2,1,0:T(8,128)(2,1)} %bitcast.5), calls=%async_computation | async-start | bytes 2097152 | tf_op jit(solution)/shard_map/all_to_all | solution.py:48
  20.8 72.1 %reduce-scatter.2.cloned.1.call-start = ((), (), s32[]{:S(2)}) async-start(), calls=%async_computation.3 | async-start | bytes 2621440 | tf_op jit(solution)/shard_map/reduce_scatter | solution.py:69
  23.1 1.2 %copy-start.1 = (s32[128]{0:T(128)S(1)}, s32[128]{0:T(128)}, u32[]{:S(2)}) copy-start(s32[128]{0:T(128)} %param.13) | copy-start | bytes 1540
  23.1 1.9 %copy-start.2 = (s32[128]{0:T(128)S(1)}, s32[128]{0:T(128)}, u32[]{:S(2)}) copy-start(s32[128]{0:T(128)} %param.11) | copy-start | bytes 1540
  23.1 2.6 %copy-start.3 = (s32[128]{0:T(128)S(1)}, s32[128]{0:T(128)}, u32[]{:S(2)}) copy-start(s32[128]{0:T(128)} %param.12) | copy-start | bytes 1540
  46.6 1.0 copy-start.4
Sparse Core Ops, SparseCore 0:
  8.9 25.2 all-gather.1
  62.9 30.0 reduce-scatter.1
where the time goes:
time: 100 us; the launch traced here: 99.8 us
  waiting for transfers between devices  46.1 us (46%)
  local copies, waits for them, and re-layouts  15.9 us (16%)
  other arithmetic  14.3 us (14%)
  between operations  13.5 us (14%)
  starting transfers between devices  7.35 us (7%)
  matrix products  2.57 us (3%)
    reduce_scatter x1, waiting for transfers between devices, shards(): lax.psum_scatter(running.reshape(block_count * tile_size, tile_size).asty...  30.2 us
    all_to_all x1, waiting for transfers between devices, shards(): lax.all_to_all(outgoing, 'env', split_axis=0, concat_axis=0, tiled=True)  9.13 us
    all_to_all x1, starting transfers between devices, shards(): lax.all_to_all(outgoing, 'env', split_axis=0, concat_axis=0, tiled=True)  7.31 us
    scatter-add x1, other arithmetic, contribute(): return running.at[target_rows].add(term_image)  6.22 us
    all_gather x1, waiting for transfers between devices, shards(): gathered = lax.all_gather(wavefunction, 'grp', axis=0, tiled=True)  6.05 us
    convert_element_type x1, other arithmetic, shards(): running.reshape(block_count * tile_size, tile_size).astype(jnp.bfloat16)  3.9 us
    gather x1, local copies, waits for them, and re-layouts, contribute(): source_blocks = blocks[source_rows]  3.25 us
    gather x1, local copies, waits for them, and re-layouts, shards(): outgoing = left_tiles[outgoing_pick]  2.7 us
  transfers between devices with their start and end apart: 3, of which 3 were waited for; matrix products, arithmetic and copies ran while one was open for 17% of the time, Pallas kernels for 0%

commit v1 on v0

v1 whole, which is shorter than its diff:
```python
import functools

import jax
import jax.numpy as jnp
from jax import lax
from jax.experimental import pallas as pl
from jax.experimental.pallas import tpu as pltpu
from jax.sharding import PartitionSpec as P

MAXS = 4
MESH = pl.DeviceIdType.MESH


def remote(src, dst, send_sem, recv_sem, where):
    return pltpu.make_async_remote_copy(
        src_ref=src,
        dst_ref=dst,
        send_sem=send_sem,
        recv_sem=recv_sem,
        device_id=where,
        device_id_type=MESH,
    )


def exchange_kernel(
    ng,
    ne,
    meta_ref,
    meta_any,
    column_ref,
    wave_ref,
    left_ref,
    gathered_ref,
    tiles_ref,
    partner_meta_ref,
    slots_ref,
    outgoing,
    meta_two,
    a2a_send,
    a2a_recv,
    fwd_send,
    fwd_recv,
    ag_send,
    ag_recv,
    agf_send,
    agf_recv,
    own_send,
    own_recv,
    local_sem,
):
    g = lax.axis_index("grp")
    e = lax.axis_index("env")
    chips = ng // 2
    core = lax.rem(g, 2)
    chip = lax.div(g, 2)
    partner = chip * 2 + 1 - core
    tiles_dev = left_ref.shape[0]
    bpd = wave_ref.shape[0]
    tg = tiles_dev * ne

    barrier = pltpu.get_barrier_semaphore()

    def greet_env(d, c):
        pl.semaphore_signal(
            barrier, inc=1, device_id={"grp": g, "env": lax.rem(e + d, ne)}, device_id_type=MESH
        )
        return c

    def greet_chip(d, c):
        pl.semaphore_signal(
            barrier,
            inc=1,
            device_id={"grp": lax.rem(chip + d, chips) * 2 + core, "env": e},
            device_id_type=MESH,
        )
        return c

    lax.fori_loop(1, ne, greet_env, 0)
    lax.fori_loop(1, chips, greet_chip, 0)
    pl.semaphore_signal(barrier, inc=1, device_id={"grp": partner, "env": e}, device_id_type=MESH)

    def ranked(read, wanted):
        packed, weight, count = jnp.int32(0), jnp.int32(1), jnp.int32(0)
        for t in range(tiles_dev):
            hit = read(t) == wanted
            packed = packed + jnp.where(hit, t * weight, 0)
            weight = jnp.where(hit, weight * tiles_dev, weight)
            count = count + jnp.where(hit, 1, 0)
        picks = []
        for s in range(MAXS):
            picks.append(lax.rem(packed, tiles_dev))
            packed = lax.div(packed, tiles_dev)
        return picks, count

    def choose(c, carry):
        base = 3 * tg + e * tiles_dev
        picks, _ = ranked(lambda t: meta_ref[base + t], column_ref[c])
        for s in range(MAXS):
            outgoing[c, s] = left_ref[picks[s]]
        return carry

    lax.fori_loop(0, ne, choose, 0)

    pl.semaphore_wait(barrier, ne - 1 + chips)

    there = {"grp": partner, "env": e}

    def a2a(d):
        return remote(
            outgoing.at[lax.rem(e + d, ne)],
            tiles_ref.at[0, e],
            a2a_send.at[d],
            a2a_recv.at[d],
            {"grp": g, "env": lax.rem(e + d, ne)},
        )

    def a2a_in(d):
        src = lax.rem(e + ne - d, ne)
        return remote(
            outgoing.at[src],
            tiles_ref.at[0, src],
            a2a_send.at[d],
            a2a_recv.at[d],
            {"grp": g, "env": lax.rem(e + d, ne)},
        )

    def forward(d):
        src = lax.rem(e + ne - d, ne)
        return remote(
            tiles_ref.at[0, src], tiles_ref.at[1, src], fwd_send.at[d], fwd_recv.at[d], there
        )

    def ag(d):
        return remote(
            wave_ref,
            gathered_ref.at[g],
            ag_send.at[d],
            ag_recv.at[d],
            {"grp": lax.rem(chip + d, chips) * 2 + core, "env": e},
        )

    def ag_in(d):
        src = lax.rem(chip + chips - d, chips) * 2 + core
        return remote(
            wave_ref,
            gathered_ref.at[src],
            ag_send.at[d],
            ag_recv.at[d],
            {"grp": lax.rem(chip + d, chips) * 2 + core, "env": e},
        )

    def ag_forward(d):
        src = lax.rem(chip + chips - d, chips) * 2 + core
        return remote(
            gathered_ref.at[src], gathered_ref.at[src], agf_send.at[d], agf_recv.at[d], there
        )

    def ag_forward_in(d):
        src = lax.rem(chip + chips - d, chips) * 2 + 1 - core
        return remote(
            gathered_ref.at[src], gathered_ref.at[src], agf_send.at[d], agf_recv.at[d], there
        )

    def loop(low, high, act):
        def step(d, c):
            act(d)
            return c

        lax.fori_loop(low, high, step, 0)

    loop(1, ne, lambda d: a2a(d).start())
    loop(1, chips, lambda d: ag(d).start())
    own_meta = remote(meta_any, partner_meta_ref, own_send.at[0], own_recv.at[0], there)
    own_meta.start()
    own_wave = remote(wave_ref, gathered_ref.at[g], own_send.at[1], own_recv.at[1], there)
    own_wave.start()
    own_wave_in = remote(wave_ref, gathered_ref.at[partner], own_send.at[1], own_recv.at[1], there)
    own_tiles = remote(
        outgoing.at[e], tiles_ref.at[1, e], own_send.at[2], own_recv.at[2], there
    )
    own_tiles.start()
    keep_wave = pltpu.make_async_copy(wave_ref, gathered_ref.at[g], local_sem.at[0])
    keep_wave.start()
    keep_tiles = pltpu.make_async_copy(outgoing.at[e], tiles_ref.at[0, e], local_sem.at[1])
    keep_tiles.start()

    own_meta.wait_recv()
    fetch = pltpu.make_async_copy(partner_meta_ref, meta_two, local_sem.at[2])
    fetch.start()
    fetch.wait()
    wanted = column_ref[e]

    def list_slots(half, table):
        def block(b, carry):
            base = b * tiles_dev
            picks, count = ranked(lambda t: table[3 * tg + base + t], wanted)
            for s in range(MAXS):
                term = base + picks[s]
                target = table[tg + term]
                owner = lax.div(target, bpd)
                row = lax.div(owner, 2) * bpd + lax.rem(target, bpd)
                mine = (lax.rem(owner, 2) == core) & (count > s)
                place = (half * ne + b) * MAXS + s
                slots_ref[0, place] = jnp.where(mine, row, -1)
                slots_ref[1, place] = table[term]
                slots_ref[2, place] = table[2 * tg + term]
            return carry

        lax.fori_loop(0, ne, block, 0)

    list_slots(0, meta_ref)
    list_slots(1, meta_two)

    def pass_on(d):
        a2a_in(d).wait_recv()
        forward(d).start()

    def pass_wave(d):
        ag_in(d).wait_recv()
        ag_forward(d).start()

    half = 1 + ne // 2
    loop(1, half, pass_on)
    loop(1, chips, pass_wave)
    loop(half, ne, pass_on)

    loop(1, ne, lambda d: forward(d).wait_recv())
    loop(1, chips, lambda d: ag_forward_in(d).wait_recv())
    own_wave_in.wait_recv()
    own_tiles.wait_recv()
    keep_wave.wait()
    keep_tiles.wait()
    loop(1, ne, lambda d: a2a(d).wait_send())
    loop(1, ne, lambda d: forward(d).wait_send())
    loop(1, chips, lambda d: ag(d).wait_send())
    loop(1, chips, lambda d: ag_forward(d).wait_send())
    own_meta.wait_send()
    own_wave.wait_send()
    own_tiles.wait_send()


UNROLL = 4


def term_kernel(slots_ref, gathered_ref, tiles_ref, right_ref, out_ref, total, listed):
    rows = out_ref.shape[0]
    places = slots_ref.shape[1]
    total[...] = jnp.zeros_like(total)

    def collect(i, n):
        row = slots_ref[0, i]
        listed[0, n] = row
        listed[1, n] = slots_ref[1, i]
        listed[2, n] = slots_ref[2, i]
        listed[3, n] = i
        return n + jnp.where(row >= 0, 1, 0)

    n = lax.fori_loop(0, places, collect, jnp.int32(0))
    for u in range(UNROLL):
        listed[0, n + u] = rows
        listed[1, n + u] = 0
        listed[2, n + u] = 0
        listed[3, n + u] = 0

    def batch(i, carry):
        images = []
        for u in range(UNROLL):
            at = i * UNROLL + u
            product = jnp.dot(
                tiles_ref[listed[3, at]],
                gathered_ref[listed[1, at]],
                preferred_element_type=jnp.float32,
            ).astype(jnp.bfloat16)
            images.append(
                jnp.dot(product, right_ref[listed[2, at]], preferred_element_type=jnp.float32)
            )
        for u in range(UNROLL):
            row = listed[0, i * UNROLL + u]
            total[row] = total[row] + images[u]
        return carry

    lax.fori_loop(0, lax.div(n + UNROLL - 1, UNROLL), batch, 0)

    def finish(r, carry):
        out_ref[r] = total[r].astype(out_ref.dtype)
        return carry

    lax.fori_loop(0, rows, finish, 0)


CHUNKS = 4


def reduce_kernel(ng, part_ref, out_ref, landed, send_sem, recv_sem):
    g = lax.axis_index("grp")
    e = lax.axis_index("env")
    chips = ng // 2
    core = lax.rem(g, 2)
    chip = lax.div(g, 2)
    size = part_ref.shape[1] // CHUNKS

    barrier = pltpu.get_barrier_semaphore()
    for d in range(1, chips):
        to = lax.rem(chip + d, chips) * 2 + core
        pl.semaphore_signal(barrier, inc=1, device_id={"grp": to, "env": e}, device_id_type=MESH)
    pl.semaphore_wait(barrier, chips - 1)

    def move(c, d):
        to = lax.rem(chip + d, chips)
        piece = pl.ds(c * size, size)
        return remote(
            part_ref.at[to, piece],
            landed.at[d, piece],
            send_sem.at[c, d],
            recv_sem.at[c, d],
            {"grp": to * 2 + core, "env": e},
        )

    for c in range(CHUNKS):
        for d in range(1, chips):
            move(c, d).start()
    for c in range(CHUNKS):
        piece = pl.ds(c * size, size)
        summed = part_ref[chip, piece].astype(jnp.float32)
        for d in range(1, chips):
            move(c, d).wait_recv()
            summed = summed + landed[d, piece].astype(jnp.float32)
        out_ref[piece] = summed.astype(out_ref.dtype)
    for c in range(CHUNKS):
        for d in range(1, chips):
            move(c, d).wait_send()


def shards(
    wavefunction,
    left_tiles,
    right_tiles,
    term_source,
    term_target,
    right_index,
    term_sector,
    column_sector,
):
    tile = left_tiles.shape[1]
    tiles_dev = left_tiles.shape[0]
    ne = lax.axis_size("env")
    ng = lax.axis_size("grp")
    chips = ng // 2
    rows_dev = wavefunction.shape[0]
    bpd = rows_dev // tile
    meta = jnp.concatenate([term_source, term_target, right_index, term_sector[:, 0]])
    wave = wavefunction.reshape(bpd, tile, tile)
    bf16 = jnp.bfloat16
    vmem = pl.BlockSpec(memory_space=pltpu.VMEM)
    smem = pl.BlockSpec(memory_space=pltpu.SMEM)
    anywhere = pl.BlockSpec(memory_space=pl.ANY)
    places = 2 * ne * MAXS
    dma = pltpu.SemaphoreType.DMA

    gathered, tiles, _, slots = pl.pallas_call(
        functools.partial(exchange_kernel, ng, ne),
        out_shape=(
            jax.ShapeDtypeStruct((ng, bpd, tile, tile), bf16),
            jax.ShapeDtypeStruct((2, ne, MAXS, tile, tile), bf16),
            jax.ShapeDtypeStruct(meta.shape, jnp.int32),
            jax.ShapeDtypeStruct((3, places), jnp.int32),
        ),
        in_specs=[smem, anywhere, smem, vmem, vmem],
        out_specs=(anywhere, anywhere, anywhere, smem),
        scratch_shapes=[
            pltpu.VMEM((ne, MAXS, tile, tile), bf16),
            pltpu.SMEM(meta.shape, jnp.int32),
            dma((ne,)),
            dma((ne,)),
            dma((ne,)),
            dma((ne,)),
            dma((chips,)),
            dma((chips,)),
            dma((chips,)),
            dma((chips,)),
            dma((3,)),
            dma((3,)),
            dma((3,)),
        ],
        compiler_params=pltpu.CompilerParams(collective_id=0, has_side_effects=True),
        name="exchange",
    )(meta, meta, column_sector, wave, left_tiles)

    part = pl.pallas_call(
        term_kernel,
        out_shape=jax.ShapeDtypeStruct((chips * bpd, tile, tile), bf16),
        in_specs=[smem, vmem, vmem, vmem],
        out_specs=vmem,
        scratch_shapes=[
            pltpu.VMEM((chips * bpd + 1, tile, tile), jnp.float32),
            pltpu.SMEM((4, places + UNROLL), jnp.int32),
        ],
        name="terms",
    )(
        slots,
        gathered.reshape(ng * bpd, tile, tile),
        tiles.reshape(places, tile, tile),
        right_tiles,
    )

    return pl.pallas_call(
        functools.partial(reduce_kernel, ng),
        out_shape=jax.ShapeDtypeStruct((rows_dev, tile), bf16),
        in_specs=[vmem],
        out_specs=vmem,
        scratch_shapes=[
            pltpu.VMEM((chips, rows_dev, tile), bf16),
            dma((CHUNKS, chips)),
            dma((CHUNKS, chips)),
        ],
        compiler_params=pltpu.CompilerParams(collective_id=1, has_side_effects=True),
        name="reduce",
    )(part.reshape(chips, rows_dev, tile))


def solution(mesh):
    placed = (
        P("grp", "env"),
        P(("grp", "env"), None, None),
        P(None, "env", None),
        P("grp"),
        P("grp"),
        P("grp"),
        P("grp", None),
        P(),
    )
    return jax.shard_map(
        shards, mesh=mesh, in_specs=placed, out_specs=P("grp", "env"), check_vma=False
    )
```

time: 100 us -> 56.1 us (0.56)
  the two profiles are of different devices: /device:TPU:0 before, /device:TPU:12 now
where the time goes in v1:
time: 56.1 us; the launch traced here: 56.2 us
  Pallas kernels  53 us (94%)
  local copies, waits for them, and re-layouts  1.87 us (3%)
  other arithmetic  1.29 us (2%)
    pallas_call x1, Pallas kernels, shards(): pl.pallas_call(functools.partial(exchange_kernel, ng, ne), out_shape=(jax...  30.7 us
    pallas_call x1, Pallas kernels, shards(): pl.pallas_call(functools.partial(reduce_kernel, ng), out_shape=jax.ShapeD...  16.8 us
    pallas_call x1, Pallas kernels, shards(): pl.pallas_call(term_kernel, out_shape=jax.ShapeDtypeStruct((chips * bpd,...  5.51 us
    unnamed x1, local copies, waits for them, and re-layouts  1.87 us
    concatenate x1, other arithmetic, shards(): jnp.concatenate([term_source, term_target, right_index, term_sector[:, 0]])  1.29 us

profile of v1, /device:TPU:12, one launch (start us, length us, event | category | flops | bytes accessed | tf_op | source)
XLA Modules:
  0.0 56.2 jit_solution(2479623562867086514)
XLA Ops:
  0.0 1.3 %pad_add_fusion.meta_ref.meta_any = s32[512]{0:T(512)} fusion(s32[128]{0:T(128)} %bitcast.9, s32[128]{0:T(128)} %param.13, s32[128]{0:T(128)} %param.12, s32[128]{0:T(128)} %param.11), kind=kLoop, calls=%fused_computation | loop fusion | flops 1536 | bytes 4096 | tf_op jit(solution)/shard_map/concatenate | solution.py:351
  1.3 30.7 %exchange.1 = (bf16[4,16,128,128]{3,2,1,0:T(8,128)(2,1)}, bf16[2,8,4,128,128]{4,3,2,1,0:T(8,128)(2,1)}, s32[512]{0:T(512)}, s32[3,64]{1,0:T(4,128)}) custom-call(s32[512]{0:T(512)} %pad_add_fusion.meta_ref.meta_any, s32[512]{0:T(512)} %pad_add_fusion.meta_ref.meta_any, s32[8]{0:T(128)} %column_ref.1, bf16[16,128,128]{2,1,0:T(8,128)(2,1)} %bitcast.8, ...), custom_call_target="tpu_custom_call" | custom-call | tf_op jit(solution)/shard_map/exchange/pallas_call | solution.py:360
  32.0 5.5 %terms.1 = bf16[32,128,128]{2,1,0:T(8,128)(2,1)} custom-call(s32[3,64]{1,0:T(4,128)} %get-tuple-element.8.slots_ref, bf16[64,128,128]{2,1,0:T(8,128)(2,1)} %bitcast.6, bf16[64,128,128]{2,1,0:T(8,128)(2,1)} %bitcast.7, bf16[26,128,128]{2,1,0:T(8,128)(2,1)} %right_ref.1), custom_call_target="tpu_custom_call" | custom-call | tf_op jit(solution)/shard_map/terms/pallas_call | solution.py:389
  37.5 16.8 %reduce.1 = bf16[2048,128]{1,0:T(8,128)(2,1)} custom-call(bf16[2,2048,128]{2,1,0:T(8,128)(2,1)} %bitcast.5), custom_call_target="tpu_custom_call" | custom-call | tf_op jit(solution)/shard_map/reduce/pallas_call | solution.py:406
  54.3 1.9 %copy.10 = bf16[2048,128]{1,0:T(8,128)(2,1)} copy(bf16[2048,128]{1,0:T(8,128)(2,1)} %reduce.1) | data formatting | bytes 1048576

commit v2 on v1

--- a/solution.py
+++ b/solution.py
@@ -25,17 +25,29 @@
 def exchange_kernel(
     ng,
     ne,
-    meta_ref,
-    meta_any,
+    src_ref,
+    tgt_ref,
+    mpo_ref,
+    sec_ref,
+    src_any,
+    tgt_any,
+    mpo_any,
+    sec_any,
     column_ref,
     wave_ref,
     left_ref,
     gathered_ref,
     tiles_ref,
-    partner_meta_ref,
+    src_far,
+    tgt_far,
+    mpo_far,
+    sec_far,
     slots_ref,
     outgoing,
-    meta_two,
+    src_two,
+    tgt_two,
+    mpo_two,
+    sec_two,
     a2a_send,
     a2a_recv,
     fwd_send,
@@ -54,15 +66,23 @@
     core = lax.rem(g, 2)
     chip = lax.div(g, 2)
     partner = chip * 2 + 1 - core
+
+    def mate(d):
+        other, bit = jnp.int32(0), 1
+        while bit < ne:
+            ours, step = lax.rem(lax.div(e, bit), 2), lax.rem(lax.div(d, bit), 2)
+            other = other + lax.rem(ours + step, 2) * bit
+            bit *= 2
+        return other
+
     tiles_dev = left_ref.shape[0]
     bpd = wave_ref.shape[0]
-    tg = tiles_dev * ne
 
     barrier = pltpu.get_barrier_semaphore()
 
     def greet_env(d, c):
         pl.semaphore_signal(
-            barrier, inc=1, device_id={"grp": g, "env": lax.rem(e + d, ne)}, device_id_type=MESH
+            barrier, inc=1, device_id={"grp": g, "env": mate(d)}, device_id_type=MESH
         )
         return c
 
@@ -93,8 +113,8 @@
         return picks, count
 
     def choose(c, carry):
-        base = 3 * tg + e * tiles_dev
-        picks, _ = ranked(lambda t: meta_ref[base + t], column_ref[c])
+        base = e * tiles_dev
+        picks, _ = ranked(lambda t: sec_ref[base + t], column_ref[c])
         for s in range(MAXS):
             outgoing[c, s] = left_ref[picks[s]]
         return carry
@@ -107,25 +127,25 @@
 
     def a2a(d):
         return remote(
-            outgoing.at[lax.rem(e + d, ne)],
+            outgoing.at[mate(d)],
             tiles_ref.at[0, e],
             a2a_send.at[d],
             a2a_recv.at[d],
-            {"grp": g, "env": lax.rem(e + d, ne)},
+            {"grp": g, "env": mate(d)},
         )
 
     def a2a_in(d):
-        src = lax.rem(e + ne - d, ne)
+        src = mate(d)
         return remote(
             outgoing.at[src],
             tiles_ref.at[0, src],
             a2a_send.at[d],
             a2a_recv.at[d],
-            {"grp": g, "env": lax.rem(e + d, ne)},
+            {"grp": g, "env": mate(d)},
         )
 
     def forward(d):
-        src = lax.rem(e + ne - d, ne)
+        src = mate(d)
         return remote(
             tiles_ref.at[0, src], tiles_ref.at[1, src], fwd_send.at[d], fwd_recv.at[d], there
         )
@@ -170,8 +190,13 @@
 
     loop(1, ne, lambda d: a2a(d).start())
     loop(1, chips, lambda d: ag(d).start())
-    own_meta = remote(meta_any, partner_meta_ref, own_send.at[0], own_recv.at[0], there)
-    own_meta.start()
+    far = (src_far, tgt_far, mpo_far, sec_far)
+    own_meta = [
+        remote(mine, theirs, own_send.at[3 + i], own_recv.at[3 + i], there)
+        for i, (mine, theirs) in enumerate(zip((src_any, tgt_any, mpo_any, sec_any), far))
+    ]
+    for copy in own_meta:
+        copy.start()
     own_wave = remote(wave_ref, gathered_ref.at[g], own_send.at[1], own_recv.at[1], there)
     own_wave.start()
     own_wave_in = remote(wave_ref, gathered_ref.at[partner], own_send.at[1], own_recv.at[1], there)
@@ -184,32 +209,36 @@
     keep_tiles = pltpu.make_async_copy(outgoing.at[e], tiles_ref.at[0, e], local_sem.at[1])
     keep_tiles.start()
 
-    own_meta.wait_recv()
-    fetch = pltpu.make_async_copy(partner_meta_ref, meta_two, local_sem.at[2])
-    fetch.start()
-    fetch.wait()
+    two = (src_two, tgt_two, mpo_two, sec_two)
+    fetches = []
+    for i in range(4):
+        own_meta[i].wait_recv()
+        fetches.append(pltpu.make_async_copy(far[i], two[i], local_sem.at[2 + i]))
+        fetches[i].start()
+    for fetch in fetches:
+        fetch.wait()
     wanted = column_ref[e]
 
-    def list_slots(half, table):
+    def list_slots(half, source, goal, mpo, sector):
         def block(b, carry):
             base = b * tiles_dev
-            picks, count = ranked(lambda t: table[3 * tg + base + t], wanted)
+            picks, count = ranked(lambda t: sector[base + t], wanted)
             for s in range(MAXS):
                 term = base + picks[s]
-                target = table[tg + term]
+                target = goal[term]
                 owner = lax.div(target, bpd)
-                row = lax.div(owner, 2) * bpd + lax.rem(target, bpd)
+                row = lax.rem(lax.div(owner, 2) + chips - chip, chips) * bpd + lax.rem(target, bpd)
                 mine = (lax.rem(owner, 2) == core) & (count > s)
                 place = (half * ne + b) * MAXS + s
                 slots_ref[0, place] = jnp.where(mine, row, -1)
-                slots_ref[1, place] = table[term]
-                slots_ref[2, place] = table[2 * tg + term]
+                slots_ref[1, place] = source[term]
+                slots_ref[2, place] = mpo[term]
             return carry
 
         lax.fori_loop(0, ne, block, 0)
 
-    list_slots(0, meta_ref)
-    list_slots(1, meta_two)
+    list_slots(0, src_ref, tgt_ref, mpo_ref, sec_ref)
+    list_slots(1, *two)
 
     def pass_on(d):
         a2a_in(d).wait_recv()
@@ -234,7 +263,8 @@
     loop(1, ne, lambda d: forward(d).wait_send())
     loop(1, chips, lambda d: ag(d).wait_send())
     loop(1, chips, lambda d: ag_forward(d).wait_send())
-    own_meta.wait_send()
+    for copy in own_meta:
+        copy.wait_send()
     own_wave.wait_send()
     own_tiles.wait_send()
 
@@ -242,8 +272,9 @@
 UNROLL = 4
 
 
-def term_kernel(slots_ref, gathered_ref, tiles_ref, right_ref, out_ref, total, listed):
-    rows = out_ref.shape[0]
+def term_kernel(slots_ref, gathered_ref, tiles_ref, right_ref, own_ref, away_ref, total, listed):
+    here = own_ref.shape[0]
+    rows = here + away_ref.shape[0]
     places = slots_ref.shape[1]
     total[...] = jnp.zeros_like(total)
 
@@ -281,54 +312,45 @@
 
     lax.fori_loop(0, lax.div(n + UNROLL - 1, UNROLL), batch, 0)
 
-    def finish(r, carry):
-        out_ref[r] = total[r].astype(out_ref.dtype)
+    def keep(r, carry):
+        own_ref[r] = total[r].astype(own_ref.dtype)
         return carry
 
-    lax.fori_loop(0, rows, finish, 0)
-
-
-CHUNKS = 4
-
-
-def reduce_kernel(ng, part_ref, out_ref, landed, send_sem, recv_sem):
+    def hand_out(r, carry):
+        away_ref[r] = total[here + r].astype(away_ref.dtype)
+        return carry
+
+    lax.fori_loop(0, here, keep, 0)
+    lax.fori_loop(0, rows - here, hand_out, 0)
+
+
+def reduce_kernel(ng, away_ref, landed_ref, send_sem, recv_sem):
     g = lax.axis_index("grp")
     e = lax.axis_index("env")
     chips = ng // 2
     core = lax.rem(g, 2)
     chip = lax.div(g, 2)
-    size = part_ref.shape[1] // CHUNKS
+
+    def there(d):
+        return {"grp": lax.rem(chip + d, chips) * 2 + core, "env": e}
 
     barrier = pltpu.get_barrier_semaphore()
     for d in range(1, chips):
-        to = lax.rem(chip + d, chips) * 2 + core
-        pl.semaphore_signal(barrier, inc=1, device_id={"grp": to, "env": e}, device_id_type=MESH)
+        pl.semaphore_signal(barrier, inc=1, device_id=there(d), device_id_type=MESH)
     pl.semaphore_wait(barrier, chips - 1)
 
-    def move(c, d):
-        to = lax.rem(chip + d, chips)
-        piece = pl.ds(c * size, size)
-        return remote(
-            part_ref.at[to, piece],
-            landed.at[d, piece],
-            send_sem.at[c, d],
-            recv_sem.at[c, d],
-            {"grp": to * 2 + core, "env": e},
-        )
-
-    for c in range(CHUNKS):
-        for d in range(1, chips):
-            move(c, d).start()
-    for c in range(CHUNKS):
-        piece = pl.ds(c * size, size)
-        summed = part_ref[chip, piece].astype(jnp.float32)
-        for d in range(1, chips):
-            move(c, d).wait_recv()
-            summed = summed + landed[d, piece].astype(jnp.float32)
-        out_ref[piece] = summed.astype(out_ref.dtype)
-    for c in range(CHUNKS):
-        for d in range(1, chips):
-            move(c, d).wait_send()
+    moves = [
+        remote(
+            away_ref.at[d - 1], landed_ref.at[d - 1], send_sem.at[d], recv_sem.at[d], there(d)
+        )
+        for d in range(1, chips)
+    ]
+    for move in moves:
+        move.start()
+    for move in moves:
+        move.wait_recv()
+    for move in moves:
+        move.wait_send()
 
 
 def shards(
@@ -348,7 +370,10 @@
     chips = ng // 2
     rows_dev = wavefunction.shape[0]
     bpd = rows_dev // tile
-    meta = jnp.concatenate([term_source, term_target, right_index, term_sector[:, 0]])
+    meta = (term_source, term_target, right_index, term_sector[:, 0])
+    listing = jax.ShapeDtypeStruct(term_source.shape, jnp.int32)
+    tile_bytes = tile * tile * 2
+    spare = 4 << 20
     wave = wavefunction.reshape(bpd, tile, tile)
     bf16 = jnp.bfloat16
     vmem = pl.BlockSpec(memory_space=pltpu.VMEM)
@@ -357,19 +382,22 @@
     places = 2 * ne * MAXS
     dma = pltpu.SemaphoreType.DMA
 
-    gathered, tiles, _, slots = pl.pallas_call(
+    gathered, tiles, *_, slots = pl.pallas_call(
         functools.partial(exchange_kernel, ng, ne),
         out_shape=(
             jax.ShapeDtypeStruct((ng, bpd, tile, tile), bf16),
             jax.ShapeDtypeStruct((2, ne, MAXS, tile, tile), bf16),
-            jax.ShapeDtypeStruct(meta.shape, jnp.int32),
+            listing,
+            listing,
+            listing,
+            listing,
             jax.ShapeDtypeStruct((3, places), jnp.int32),
         ),
-        in_specs=[smem, anywhere, smem, vmem, vmem],
-        out_specs=(anywhere, anywhere, anywhere, smem),
+        in_specs=[smem] * 4 + [anywhere] * 4 + [smem, vmem, vmem],
+        out_specs=(anywhere,) * 6 + (smem,),
         scratch_shapes=[
             pltpu.VMEM((ne, MAXS, tile, tile), bf16),
-            pltpu.SMEM(meta.shape, jnp.int32),
+            *[pltpu.SMEM(listing.shape, jnp.int32) for _ in range(4)],
             dma((ne,)),
             dma((ne,)),
             dma((ne,)),
@@ -378,23 +406,34 @@
             dma((chips,)),
             dma((chips,)),
             dma((chips,)),
-            dma((3,)),
-            dma((3,)),
-            dma((3,)),
+            dma((7,)),
+            dma((7,)),
+            dma((6,)),
         ],
-        compiler_params=pltpu.CompilerParams(collective_id=0, has_side_effects=True),
+        compiler_params=pltpu.CompilerParams(
+            collective_id=0,
+            has_side_effects=True,
+            vmem_limit_bytes=spare + tile_bytes * (bpd + tiles_dev + ne * MAXS),
+        ),
         name="exchange",
-    )(meta, meta, column_sector, wave, left_tiles)
-
-    part = pl.pallas_call(
+    )(*meta, *meta, column_sector, wave, left_tiles)
+
+    own, away = pl.pallas_call(
         term_kernel,
-        out_shape=jax.ShapeDtypeStruct((chips * bpd, tile, tile), bf16),
+        out_shape=(
+            jax.ShapeDtypeStruct((bpd, tile, tile), bf16),
+            jax.ShapeDtypeStruct(((chips - 1) * bpd, tile, tile), bf16),
+        ),
         in_specs=[smem, vmem, vmem, vmem],
-        out_specs=vmem,
+        out_specs=(vmem, vmem),
         scratch_shapes=[
             pltpu.VMEM((chips * bpd + 1, tile, tile), jnp.float32),
             pltpu.SMEM((4, places + UNROLL), jnp.int32),
         ],
+        compiler_params=pltpu.CompilerParams(
+            vmem_limit_bytes=spare
+            + tile_bytes * (ng * bpd + places + right_tiles.shape[0] + 3 * chips * bpd + 2)
+        ),
         name="terms",
     )(
         slots,
@@ -403,19 +442,21 @@
         right_tiles,
     )
 
-    return pl.pallas_call(
+    landed = pl.pallas_call(
         functools.partial(reduce_kernel, ng),
-        out_shape=jax.ShapeDtypeStruct((rows_dev, tile), bf16),
-        in_specs=[vmem],
-        out_specs=vmem,
-        scratch_shapes=[
-            pltpu.VMEM((chips, rows_dev, tile), bf16),
-            dma((CHUNKS, chips)),
-            dma((CHUNKS, chips)),
-        ],
-        compiler_params=pltpu.CompilerParams(collective_id=1, has_side_effects=True),
+        out_shape=jax.ShapeDtypeStruct((chips - 1, rows_dev, tile), bf16),
+        in_specs=[anywhere],
+        out_specs=anywhere,
+        scratch_shapes=[dma((chips,)), dma((chips,))],
+        compiler_params=pltpu.CompilerParams(
+            collective_id=1, has_side_effects=True, vmem_limit_bytes=spare
+        ),
         name="reduce",
-    )(part.reshape(chips, rows_dev, tile))
+    )(away.reshape(chips - 1, rows_dev, tile))
+    summed = own.reshape(rows_dev, tile).astype(jnp.float32)
+    for d in range(chips - 1):
+        summed = summed + landed[d].astype(jnp.float32)
+    return summed.astype(bf16)
 
 
 def solution(mesh):

time: 56.1 us -> 54.4 us (0.970)
  Pallas kernels: 53 us -> 46.5 us
  local copies, waits for them, and re-layouts: 1.87 us -> 6.51 us
    unnamed x1 -> x16, local copies, waits for them, and re-layouts: 1.87 us -> 6.51 us
    pallas_call x1, Pallas kernels: 5.51 us -> 2.01 us  [shards(): pl.pallas_call(term_kernel, out_shape=(jax.ShapeDtypeStruct((bpd, tile, t...]
    pallas_call x1, Pallas kernels: 16.8 us -> 14.7 us  [shards(): pl.pallas_call(functools.partial(reduce_kernel, ng), out_shape=jax.ShapeD...]
    concatenate x1 -> x0, other arithmetic: 1.29 us -> none  [shards(): jnp.concatenate([term_source, term_target, right_index, term_sector[:, 0]])]
    convert_element_type x0 -> x1, other arithmetic: none -> 0.97 us  [shards(): return summed.astype(bf16)]
    pallas_call x1, Pallas kernels: 30.7 us -> 29.8 us  [shards(): pl.pallas_call(functools.partial(exchange_kernel, ng, ne), out_shape=(jax...]
where the time goes in v2:
time: 54.4 us; the launch traced here: 54 us
  Pallas kernels  46.5 us (85%)
  local copies, waits for them, and re-layouts  6.51 us (12%)
  other arithmetic  0.97 us (2%)
    pallas_call x1, Pallas kernels, shards(): pl.pallas_call(functools.partial(exchange_kernel, ng, ne), out_shape=(jax...  29.8 us
    pallas_call x1, Pallas kernels, shards(): pl.pallas_call(functools.partial(reduce_kernel, ng), out_shape=jax.ShapeD...  14.7 us
    unnamed x16, local copies, waits for them, and re-layouts  6.51 us
    pallas_call x1, Pallas kernels, shards(): pl.pallas_call(term_kernel, out_shape=(jax.ShapeDtypeStruct((bpd, tile, t...  2.01 us

profile of v2, /device:TPU:12, one launch (start us, length us, event | category | flops | bytes accessed | tf_op | source)
XLA Modules:
  0.0 54.0 jit_solution(2097057340132770632)
XLA Ops:
  0.0 0.0 copy-start.1
  0.0 1.0 %copy-done.1 = bf16[2048,128]{1,0:T(8,128)(2,1)S(1)} copy-done((bf16[2048,128]{1,0:T(8,128)(2,1)S(1)}, bf16[2048,128]{1,0:T(8,128)(2,1)}, u32[]{:S(2)}) %copy-start.1) | copy-done | bytes 524312
  1.0 0.0 copy-start.2
  1.0 1.0 %copy-done.2 = bf16[16,128,128]{2,1,0:T(8,128)(2,1)S(1)} copy-done((bf16[16,128,128]{2,1,0:T(8,128)(2,1)S(1)}, bf16[16,128,128]{2,1,0:T(8,128)(2,1)}, u32[]{:S(2)}) %copy-start.2) | copy-done | bytes 524312
  2.1 0.0 copy-start.3
  2.1 0.7 %copy-done.3 = s32[128]{0:T(128)S(1)} copy-done((s32[128]{0:T(128)S(1)}, s32[128]{0:T(128)}, u32[]{:S(2)}) %copy-start.3) | copy-done | bytes 536
  2.7 0.0 copy-start.4
  2.7 0.7 %copy-done.4 = s32[128]{0:T(128)S(1)} copy-done((s32[128]{0:T(128)S(1)}, s32[128]{0:T(128)}, u32[]{:S(2)}) %copy-start.4) | copy-done | bytes 536
  3.4 0.0 copy-start.5
  3.4 0.7 %copy-done.5 = s32[128]{0:T(128)S(1)} copy-done((s32[128]{0:T(128)S(1)}, s32[128]{0:T(128)}, u32[]{:S(2)}) %copy-start.5) | copy-done | bytes 536
  4.1 0.0 copy-start.6
  4.1 0.7 %copy-done.6 = s32[128,1]{0,1:T(1,128)S(1)} copy-done((s32[128,1]{0,1:T(1,128)S(1)}, s32[128,1]{0,1:T(1,128)}, u32[]{:S(2)}) %copy-start.6) | copy-done | bytes 536
  4.7 0.0 copy-start.7
  4.7 0.7 %copy-done.7 = s32[8]{0:T(128)S(1)} copy-done((s32[8]{0:T(128)S(1)}, s32[8]{0:T(128)}, u32[]{:S(2)}) %copy-start.7) | copy-done | bytes 56
  5.4 29.8 %exchange.1 = (bf16[4,16,128,128]{3,2,1,0:T(8,128)(2,1)S(1)}, bf16[2,8,4,128,128]{4,3,2,1,0:T(8,128)(2,1)S(1)}, s32[128]{0:T(128)}, s32[128]{0:T(128)}, s32[128]...) custom-call(s32[128]{0:T(128)S(1)} %copy-done.3, s32[128]{0:T(128)S(1)} %copy-done.4, s32[128]{0:T(128)S(1)} %copy-done.5, ...), custom_call_target="tpu_custom_call" | custom-call | tf_op jit(solution)/shard_map/exchange/pallas_call | solution.py:385
  35.2 0.0 copy-start
  35.2 1.1 %copy-done = bf16[26,128,128]{2,1,0:T(8,128)(2,1)S(1)} copy-done((bf16[26,128,128]{2,1,0:T(8,128)(2,1)S(1)}, bf16[26,128,128]{2,1,0:T(8,128)(2,1)}, u32[]{:S(2)}) %copy-start) | copy-done | bytes 851992
  36.3 2.0 %terms.1 = (bf16[16,128,128]{2,1,0:T(8,128)(2,1)S(1)}, bf16[16,128,128]{2,1,0:T(8,128)(2,1)S(1)}) custom-call(s32[3,64]{1,0:T(4,128)S(1)} %get-tuple-element.10.slots_ref, bf16[64,128,128]{2,1,0:T(8,128)(2,1)S(1)} %bitcast.11, bf16[64,128,128]{2,1,0:T(8,128)(2,1)S(1)} %bitcast.12, bf16[26,128,128]{2,1,0:T(8,128)(2,1)S(1)} %copy-done), custom_call_target="tpu_custom_call" | custom-call | tf_op jit(solution)/shard_map/terms/pallas_call | solution.py:421
  38.3 14.7 %reduce.1 = bf16[1,2048,128]{2,1,0:T(8,128)(2,1)S(1)} custom-call(bf16[1,2048,128]{2,1,0:T(8,128)(2,1)S(1)} %bitcast.13), custom_call_target="tpu_custom_call" | custom-call | tf_op jit(solution)/shard_map/reduce/pallas_call | solution.py:445
  53.0 1.0 %fusion = bf16[2048,128]{1,0:T(8,128)(2,1)} fusion(bf16[1,2048,128]{2,1,0:T(8,128)(2,1)S(1)} %reduce.1, bf16[16,128,128]{2,1,0:T(8,128)(2,1)S(1)} %get-tuple-element.13), kind=kLoop, calls=%fused_computation.1 | loop fusion | flops 1048576 | bytes 1572864 | tf_op jit(solution)/shard_map/convert_element_type | solution.py:459
Async XLA Ops:
  0.0 1.0 %copy-start.1 = (bf16[2048,128]{1,0:T(8,128)(2,1)S(1)}, bf16[2048,128]{1,0:T(8,128)(2,1)}, u32[]{:S(2)}) copy-start(bf16[2048,128]{1,0:T(8,128)(2,1)} %param.8) | copy-start | bytes 1572868
  1.0 1.0 %copy-start.2 = (bf16[16,128,128]{2,1,0:T(8,128)(2,1)S(1)}, bf16[16,128,128]{2,1,0:T(8,128)(2,1)}, u32[]{:S(2)}) copy-start(bf16[16,128,128]{2,1,0:T(8,128)(2,1)} %left_ref.1) | copy-start | bytes 1572868
  2.1 0.7 %copy-start.3 = (s32[128]{0:T(128)S(1)}, s32[128]{0:T(128)}, u32[]{:S(2)}) copy-start(s32[128]{0:T(128)} %src_any.1) | copy-start | bytes 1540
  2.7 0.7 %copy-start.4 = (s32[128]{0:T(128)S(1)}, s32[128]{0:T(128)}, u32[]{:S(2)}) copy-start(s32[128]{0:T(128)} %tgt_any.1) | copy-start | bytes 1540
  3.4 0.7 %copy-start.5 = (s32[128]{0:T(128)S(1)}, s32[128]{0:T(128)}, u32[]{:S(2)}) copy-start(s32[128]{0:T(128)} %mpo_any.1) | copy-start | bytes 1540
  4.1 0.7 %copy-start.6 = (s32[128,1]{0,1:T(1,128)S(1)}, s32[128,1]{0,1:T(1,128)}, u32[]{:S(2)}) copy-start(s32[128,1]{0,1:T(1,128)} %param.14) | copy-start | bytes 1540
  4.7 0.7 %copy-start.7 = (s32[8]{0:T(128)S(1)}, s32[8]{0:T(128)}, u32[]{:S(2)}) copy-start(s32[8]{0:T(128)} %column_ref.1) | copy-start | bytes 100
  35.2 1.2 %copy-start = (bf16[26,128,128]{2,1,0:T(8,128)(2,1)S(1)}, bf16[26,128,128]{2,1,0:T(8,128)(2,1)}, u32[]{:S(2)}) copy-start(bf16[26,128,128]{2,1,0:T(8,128)(2,1)} %right_ref.1) | copy-start | bytes 2555908
